TPU v7x, 256 devices: a whole 4x4x8 slice. The times are simulated.
256 devices in a mesh: group: 16 (over x_lo, y, core), dp: 16 (over x_hi, z).
Axes of the slice: x: 4 (x_hi: 2, x_lo: 2; x = x_hi * 2 + x_lo), y: 4, z: 8, core: 2. Of those that a mesh axis runs over, the one named last changes fastest.
Arguments:
- latents: bfloat16 [16, 512, 6144], P('group', 'dp'), may hold values from -6 to 6
- steps: int32 [16], P('group'), may hold values from 0 to 15
- segment_ids: int32 [512], replicated, may hold values from 0 to 15, never falling along the last dimension, each value on 1 to 64 neighbouring positions
- mod_table: float32 [16, 2, 6144], replicated, may hold values from -3 to 3
- w_query: bfloat16 [6144, 4096], P(None, 'dp')
- w_key: bfloat16 [6144, 4096], P(None, 'dp')
- w_value: bfloat16 [6144, 4096], P(None, 'dp'), may hold values from -0.3125 to 0.3125
Outputs:
- attended: bfloat16 [16, 512, 4096], P('group', 'dp')
Inputs may be any that keep to these rules, and one draw needn't show every extreme that they name: `segment_ids`: rows of one clip are contiguous; every clip index occurs, a clip holds 1 to 64 rows and one holds exactly that many.
All inputs are finite; a program needn't handle non-finite values.
Results may differ from a plain program's by a relative error of at most 0.011.
Values may be sent and summed in bfloat16 or wider, within the bound.
A program may use at most 128 MiB of HBM per device.

v0:
```python
import math

import jax
import jax.numpy as jnp
from jax import lax
from jax.sharding import PartitionSpec as P

D = 6144
HD = 128
HEAD_DEV = 2
STEPS = 16


def in_one_piece(arrays, axis, dim, along):
    both = jnp.concatenate(arrays, axis=along)
    out, at, gathered = (lax.all_gather(both, axis, axis=dim, tiled=True), 0, [])
    for a in arrays:
        gathered.append(lax.slice_in_dim(out, at, at + a.shape[along], axis=along))
        at += a.shape[along]
    return tuple(gathered)


def per_device(latents, steps, segment_ids, mod_table, w_query, w_key, w_value):
    rows_here = latents.shape[1]
    tokc = rows_here * lax.axis_size("dp")
    width = HEAD_DEV * HD
    x = latents[0].astype(jnp.float32)
    normed = x * lax.rsqrt(jnp.mean(x * x, axis=-1, keepdims=True) + 1e-06)
    picker = (steps[:, None] == jnp.arange(STEPS, dtype=jnp.int32)[None, :]).astype(jnp.float32)
    modulation = jnp.dot(picker, mod_table.reshape(STEPS, 2 * D), precision=lax.Precision.HIGHEST)
    modulated = (normed * (1.0 + modulation[:, :D]) + modulation[:, D:]).astype(jnp.bfloat16)
    piece = lax.all_gather(modulated, "dp", axis=0, tiled=True)
    first = jnp.dot(piece, w_query, preferred_element_type=jnp.float32).astype(jnp.bfloat16)
    second = jnp.dot(piece, w_key, preferred_element_type=jnp.float32).astype(jnp.bfloat16)
    third = jnp.dot(piece, w_value, preferred_element_type=jnp.float32).astype(jnp.bfloat16)
    projected = jnp.concatenate([first, second, third], axis=1)
    query = projected[:, :width].reshape(tokc, HEAD_DEV, HD)
    keys_own = projected[:, width : 2 * width]
    values_own = projected[:, 2 * width :]
    mine = lax.axis_index("group")
    same_clip = segment_ids[:, None] == segment_ids[None, :]
    inverse = 1.0 / math.sqrt(HD)

    def update(carry, key_block, value_block):
        best, total, accum = carry
        scores = (
            jnp.einsum(
                "thd,khd->htk",
                query,
                key_block.reshape(tokc, HEAD_DEV, HD),
                preferred_element_type=jnp.float32,
            )
            * inverse
        )
        scores = jnp.where(same_clip[None], scores, -1e30)
        new_best = jnp.maximum(best, jnp.max(scores, axis=-1))
        weights = jnp.where(same_clip[None], jnp.exp(scores - new_best[:, :, None]), 0.0)
        fade = jnp.exp(best - new_best)
        total = total * fade + jnp.sum(weights, axis=-1)
        added = jnp.einsum(
            "htk,khd->thd",
            weights.astype(jnp.bfloat16),
            value_block.reshape(tokc, HEAD_DEV, HD),
            preferred_element_type=jnp.float32,
        )
        accum = accum * jnp.transpose(fade)[:, :, None] + added
        return (new_best, total, accum)

    def visit(carry, key_block, value_block, source):
        usable = jnp.logical_and(source <= mine, source >= 0)
        return lax.cond(
            usable, lambda state: update(state, key_block, value_block), lambda state: state, carry
        )

    start_state = (
        jnp.full((HEAD_DEV, tokc), -1e30, jnp.float32),
        jnp.zeros((HEAD_DEV, tokc), jnp.float32),
        jnp.zeros((tokc, HEAD_DEV, HD), jnp.float32),
    )
    piece = in_one_piece((keys_own, values_own), "group", 0, 1)
    count = piece[0].shape[0] // tokc

    def single(index, state):
        key_block = lax.dynamic_slice_in_dim(piece[0], index * tokc, tokc, 0)
        value_block = lax.dynamic_slice_in_dim(piece[1], index * tokc, tokc, 0)
        return visit(state, key_block, value_block, index)

    carry = lax.fori_loop(0, count, single, start_state)
    best, total, accum = carry
    result = (accum / jnp.transpose(total)[:, :, None]).reshape(tokc, width).astype(jnp.bfloat16)
    regrouped = lax.all_to_all(result, "dp", split_axis=0, concat_axis=1, tiled=True)
    return regrouped[None]


def solution(mesh):
    placed = (
        P("group", "dp", None),
        P("group"),
        P(),
        P(),
        P(None, "dp"),
        P(None, "dp"),
        P(None, "dp"),
    )
    return jax.shard_map(
        per_device, mesh=mesh, in_specs=placed, out_specs=P("group", "dp", None), check_vma=False
    )
```

profile of v0, /device:TPU:27, one launch (start us, length us, event | category | flops | bytes accessed | tf_op | source)
XLA Modules:
  0.0 297.3 jit_solution(8042137725669814860)
XLA Ops:
  7.3 1.3 fusion.15
  8.7 1.6 copy.26
  11.7 116.8 %all-gather.3.cloned.1.call-done = bf16[512,6144]{1,0:T(8,128)(2,1)} async-done(((bf16[32,6144]{1,0:T(8,128)(2,1)}), bf16[512,6144]{1,0:T(8,128)(2,1)}) %all-gather.3.cloned.1.call-update) | async-done | bytes 6291472 | tf_op jit(solution)/shard_map/all_gather | solution.py:32
  128.5 4.8 %convolution_convert_fusion.1 = bf16[512,256]{0,1:T(8,128)(2,1)S(1)} fusion(bf16[512,6144]{1,0:T(8,128)(2,1)} %all-gather.3.cloned.1.call-done, bf16[6144,256]{1,0:T(8,128)(2,1)S(1)} %copy-done), kind=kOutput, calls=%fused_computation.22 | convolution fusion | flops 1610743808 | bytes 9699328 | tf_op jit(solution)/shard_map/dot_general | solution.py:35
  134.0 1.8 convolution_convert_fusion.2
  136.7 6.3 %convolution_convert_fusion = bf16[512,256]{0,1:T(8,128)(2,1)} fusion(bf16[512,6144]{1,0:T(8,128)(2,1)} %all-gather.3.cloned.1.call-done, bf16[6144,256]{1,0:T(8,128)(2,1)} %param.15), kind=kOutput, calls=%fused_computation.21 | convolution fusion | flops 1610743808 | bytes 9699328 | tf_op jit(solution)/shard_map/dot_general | solution.py:33
  144.1 45.9 %all-gather.5.cloned.1.call-done = bf16[8192,512]{0,1:T(8,128)(2,1)} async-done(((bf16[512,512]{0,1:T(8,128)(2,1)}), bf16[8192,512]{0,1:T(8,128)(2,1)}) %all-gather.5.cloned.1.call-update) | async-done | bytes 8388624 | tf_op jit(solution)/shard_map/all_gather | solution.py:16
  190.0 5.9 %fusion.24 = (bf16[8192,256]{0,1:T(8,128)(2,1)}, bf16[8192,256]{0,1:T(8,128)(2,1)}) fusion(bf16[8192,512]{0,1:T(8,128)(2,1)} %all-gather.5.cloned.1.call-done), kind=kLoop, calls=%fused_computation.39 | loop fusion | bytes 16777216 | tf_op jit(solution)/shard_map/slice | solution.py:18
  196.7 72.6 %while.18 = (s32[]{:T(128)}, f32[2,512]{1,0:T(2,128)S(1)}, f32[2,512]{1,0:T(2,128)S(1)}, f32[512,2,128]{2,0,1:T(8,128)}, s32[]{:T(128)}, /*index=5*/bf16[8192,25...) while((s32[]{:T(128)}, f32[2,512]{1,0:T(2,128)S(1)}, ...), condition=%wide.region_6.7_spmd.clone, body=%wide.region_1.6_spmd.clone.sunk | while | flops 275778560 | bytes 14487929 | solution.py:88
  196.7 4.5 %conditional.3 = ((f32[2,512]{1,0:T(2,128)S(1)}, f32[2,512]{1,0:T(2,128)S(1)}, f32[512,2,128]{2,0,1:T(8,128)})) conditional(s32[]{:T(128)} %convert_element_type.58, (f32[2,512]{1,0:T(2,128)S(1)}, f32[2,512]{1,0:T(2,128)S(1)}, f32[512,2,128]{2,0,1:T(8,128)}) %tuple.61, (s32[512]{0:T(512)S(1)}, s32[]{:T(128)}, bf16[8192,256]{0,1:T(8,128)(2,1)}, ...), branch_computations={%region_2.0_spmd, %region_3.5_spmd} | conditional | flops 275778560 | bytes 14487690 | solution.py:71
  196.9 1.1 constant_dynamic-slice_fusion
  201.2 4.5 %conditional.3 = ((f32[2,512]{1,0:T(2,128)S(1)}, f32[2,512]{1,0:T(2,128)S(1)}, f32[512,2,128]{2,0,1:T(8,128)})) conditional(s32[]{:T(128)} %convert_element_type.58, (f32[2,512]{1,0:T(2,128)S(1)}, f32[2,512]{1,0:T(2,128)S(1)}, f32[512,2,128]{2,0,1:T(8,128)}) %tuple.61, (s32[512]{0:T(512)S(1)}, s32[]{:T(128)}, bf16[8192,256]{0,1:T(8,128)(2,1)}, ...), branch_computations={%region_2.0_spmd, %region_3.5_spmd} | conditional | flops 275778560 | bytes 14487690 | solution.py:71
  205.7 4.5 %conditional.3 = ((f32[2,512]{1,0:T(2,128)S(1)}, f32[2,512]{1,0:T(2,128)S(1)}, f32[512,2,128]{2,0,1:T(8,128)})) conditional(s32[]{:T(128)} %convert_element_type.58, (f32[2,512]{1,0:T(2,128)S(1)}, f32[2,512]{1,0:T(2,128)S(1)}, f32[512,2,128]{2,0,1:T(8,128)}) %tuple.61, (s32[512]{0:T(512)S(1)}, s32[]{:T(128)}, bf16[8192,256]{0,1:T(8,128)(2,1)}, ...), branch_computations={%region_2.0_spmd, %region_3.5_spmd} | conditional | flops 275778560 | bytes 14487690 | solution.py:71
  206.0 1.1 constant_dynamic-slice_fusion
  210.3 4.5 %conditional.3 = ((f32[2,512]{1,0:T(2,128)S(1)}, f32[2,512]{1,0:T(2,128)S(1)}, f32[512,2,128]{2,0,1:T(8,128)})) conditional(s32[]{:T(128)} %convert_element_type.58, (f32[2,512]{1,0:T(2,128)S(1)}, f32[2,512]{1,0:T(2,128)S(1)}, f32[512,2,128]{2,0,1:T(8,128)}) %tuple.61, (s32[512]{0:T(512)S(1)}, s32[]{:T(128)}, bf16[8192,256]{0,1:T(8,128)(2,1)}, ...), branch_computations={%region_2.0_spmd, %region_3.5_spmd} | conditional | flops 275778560 | bytes 14487690 | solution.py:71
  210.5 1.1 constant_dynamic-slice_fusion
  214.8 4.5 %conditional.3 = ((f32[2,512]{1,0:T(2,128)S(1)}, f32[2,512]{1,0:T(2,128)S(1)}, f32[512,2,128]{2,0,1:T(8,128)})) conditional(s32[]{:T(128)} %convert_element_type.58, (f32[2,512]{1,0:T(2,128)S(1)}, f32[2,512]{1,0:T(2,128)S(1)}, f32[512,2,128]{2,0,1:T(8,128)}) %tuple.61, (s32[512]{0:T(512)S(1)}, s32[]{:T(128)}, bf16[8192,256]{0,1:T(8,128)(2,1)}, ...), branch_computations={%region_2.0_spmd, %region_3.5_spmd} | conditional | flops 275778560 | bytes 14487690 | solution.py:71
  219.4 4.5 %conditional.3 = ((f32[2,512]{1,0:T(2,128)S(1)}, f32[2,512]{1,0:T(2,128)S(1)}, f32[512,2,128]{2,0,1:T(8,128)})) conditional(s32[]{:T(128)} %convert_element_type.58, (f32[2,512]{1,0:T(2,128)S(1)}, f32[2,512]{1,0:T(2,128)S(1)}, f32[512,2,128]{2,0,1:T(8,128)}) %tuple.61, (s32[512]{0:T(512)S(1)}, s32[]{:T(128)}, bf16[8192,256]{0,1:T(8,128)(2,1)}, ...), branch_computations={%region_2.0_spmd, %region_3.5_spmd} | conditional | flops 275778560 | bytes 14487690 | solution.py:71
  219.6 1.1 constant_dynamic-slice_fusion
  223.9 4.5 %conditional.3 = ((f32[2,512]{1,0:T(2,128)S(1)}, f32[2,512]{1,0:T(2,128)S(1)}, f32[512,2,128]{2,0,1:T(8,128)})) conditional(s32[]{:T(128)} %convert_element_type.58, (f32[2,512]{1,0:T(2,128)S(1)}, f32[2,512]{1,0:T(2,128)S(1)}, f32[512,2,128]{2,0,1:T(8,128)}) %tuple.61, (s32[512]{0:T(512)S(1)}, s32[]{:T(128)}, bf16[8192,256]{0,1:T(8,128)(2,1)}, ...), branch_computations={%region_2.0_spmd, %region_3.5_spmd} | conditional | flops 275778560 | bytes 14487690 | solution.py:71
  224.2 1.1 constant_dynamic-slice_fusion
  228.4 4.5 %conditional.3 = ((f32[2,512]{1,0:T(2,128)S(1)}, f32[2,512]{1,0:T(2,128)S(1)}, f32[512,2,128]{2,0,1:T(8,128)})) conditional(s32[]{:T(128)} %convert_element_type.58, (f32[2,512]{1,0:T(2,128)S(1)}, f32[2,512]{1,0:T(2,128)S(1)}, f32[512,2,128]{2,0,1:T(8,128)}) %tuple.61, (s32[512]{0:T(512)S(1)}, s32[]{:T(128)}, bf16[8192,256]{0,1:T(8,128)(2,1)}, ...), branch_computations={%region_2.0_spmd, %region_3.5_spmd} | conditional | flops 275778560 | bytes 14487690 | solution.py:71
  233.0 4.5 %conditional.3 = ((f32[2,512]{1,0:T(2,128)S(1)}, f32[2,512]{1,0:T(2,128)S(1)}, f32[512,2,128]{2,0,1:T(8,128)})) conditional(s32[]{:T(128)} %convert_element_type.58, (f32[2,512]{1,0:T(2,128)S(1)}, f32[2,512]{1,0:T(2,128)S(1)}, f32[512,2,128]{2,0,1:T(8,128)}) %tuple.61, (s32[512]{0:T(512)S(1)}, s32[]{:T(128)}, bf16[8192,256]{0,1:T(8,128)(2,1)}, ...), branch_computations={%region_2.0_spmd, %region_3.5_spmd} | conditional | flops 275778560 | bytes 14487690 | solution.py:71
  237.5 4.5 %conditional.3 = ((f32[2,512]{1,0:T(2,128)S(1)}, f32[2,512]{1,0:T(2,128)S(1)}, f32[512,2,128]{2,0,1:T(8,128)})) conditional(s32[]{:T(128)} %convert_element_type.58, (f32[2,512]{1,0:T(2,128)S(1)}, f32[2,512]{1,0:T(2,128)S(1)}, f32[512,2,128]{2,0,1:T(8,128)}) %tuple.61, (s32[512]{0:T(512)S(1)}, s32[]{:T(128)}, bf16[8192,256]{0,1:T(8,128)(2,1)}, ...), branch_computations={%region_2.0_spmd, %region_3.5_spmd} | conditional | flops 275778560 | bytes 14487690 | solution.py:71
  242.1 4.5 %conditional.3 = ((f32[2,512]{1,0:T(2,128)S(1)}, f32[2,512]{1,0:T(2,128)S(1)}, f32[512,2,128]{2,0,1:T(8,128)})) conditional(s32[]{:T(128)} %convert_element_type.58, (f32[2,512]{1,0:T(2,128)S(1)}, f32[2,512]{1,0:T(2,128)S(1)}, f32[512,2,128]{2,0,1:T(8,128)}) %tuple.61, (s32[512]{0:T(512)S(1)}, s32[]{:T(128)}, bf16[8192,256]{0,1:T(8,128)(2,1)}, ...), branch_computations={%region_2.0_spmd, %region_3.5_spmd} | conditional | flops 275778560 | bytes 14487690 | solution.py:71
  246.6 4.5 %conditional.3 = ((f32[2,512]{1,0:T(2,128)S(1)}, f32[2,512]{1,0:T(2,128)S(1)}, f32[512,2,128]{2,0,1:T(8,128)})) conditional(s32[]{:T(128)} %convert_element_type.58, (f32[2,512]{1,0:T(2,128)S(1)}, f32[2,512]{1,0:T(2,128)S(1)}, f32[512,2,128]{2,0,1:T(8,128)}) %tuple.61, (s32[512]{0:T(512)S(1)}, s32[]{:T(128)}, bf16[8192,256]{0,1:T(8,128)(2,1)}, ...), branch_computations={%region_2.0_spmd, %region_3.5_spmd} | conditional | flops 275778560 | bytes 14487690 | solution.py:71
  251.1 4.5 %conditional.3 = ((f32[2,512]{1,0:T(2,128)S(1)}, f32[2,512]{1,0:T(2,128)S(1)}, f32[512,2,128]{2,0,1:T(8,128)})) conditional(s32[]{:T(128)} %convert_element_type.58, (f32[2,512]{1,0:T(2,128)S(1)}, f32[2,512]{1,0:T(2,128)S(1)}, f32[512,2,128]{2,0,1:T(8,128)}) %tuple.61, (s32[512]{0:T(512)S(1)}, s32[]{:T(128)}, bf16[8192,256]{0,1:T(8,128)(2,1)}, ...), branch_computations={%region_2.0_spmd, %region_3.5_spmd} | conditional | flops 275778560 | bytes 14487690 | solution.py:71
  255.7 4.5 %conditional.3 = ((f32[2,512]{1,0:T(2,128)S(1)}, f32[2,512]{1,0:T(2,128)S(1)}, f32[512,2,128]{2,0,1:T(8,128)})) conditional(s32[]{:T(128)} %convert_element_type.58, (f32[2,512]{1,0:T(2,128)S(1)}, f32[2,512]{1,0:T(2,128)S(1)}, f32[512,2,128]{2,0,1:T(8,128)}) %tuple.61, (s32[512]{0:T(512)S(1)}, s32[]{:T(128)}, bf16[8192,256]{0,1:T(8,128)(2,1)}, ...), branch_computations={%region_2.0_spmd, %region_3.5_spmd} | conditional | flops 275778560 | bytes 14487690 | solution.py:71
  260.2 4.5 %conditional.3 = ((f32[2,512]{1,0:T(2,128)S(1)}, f32[2,512]{1,0:T(2,128)S(1)}, f32[512,2,128]{2,0,1:T(8,128)})) conditional(s32[]{:T(128)} %convert_element_type.58, (f32[2,512]{1,0:T(2,128)S(1)}, f32[2,512]{1,0:T(2,128)S(1)}, f32[512,2,128]{2,0,1:T(8,128)}) %tuple.61, (s32[512]{0:T(512)S(1)}, s32[]{:T(128)}, bf16[8192,256]{0,1:T(8,128)(2,1)}, ...), branch_computations={%region_2.0_spmd, %region_3.5_spmd} | conditional | flops 275778560 | bytes 14487690 | solution.py:71
  264.7 4.5 %conditional.3 = ((f32[2,512]{1,0:T(2,128)S(1)}, f32[2,512]{1,0:T(2,128)S(1)}, f32[512,2,128]{2,0,1:T(8,128)})) conditional(s32[]{:T(128)} %convert_element_type.58, (f32[2,512]{1,0:T(2,128)S(1)}, f32[2,512]{1,0:T(2,128)S(1)}, f32[512,2,128]{2,0,1:T(8,128)}) %tuple.61, (s32[512]{0:T(512)S(1)}, s32[]{:T(128)}, bf16[8192,256]{0,1:T(8,128)(2,1)}, ...), branch_computations={%region_2.0_spmd, %region_3.5_spmd} | conditional | flops 275778560 | bytes 14487690 | solution.py:71
  269.3 1.2 divide_convert_fusion
  271.7 17.8 %all_to_all.13 = bf16[16,32,256]{2,1,0:T(8,128)(2,1)S(1)} all-to-all(bf16[16,32,256]{2,1,0:T(8,128)(2,1)} %convert_element_type.47), channel_id=1, replica_groups=mesh['group'=16,'dp'=16] {'dp'}, dimensions={0} | all-to-all | bytes 524288 | tf_op jit(solution)/shard_map/all_to_all | solution.py:91
  (214 shorter events, 72.2 us)
Async XLA Ops:
  6.5 121.9 %copy-start = (bf16[6144,256]{1,0:T(8,128)(2,1)S(1)}, bf16[6144,256]{1,0:T(8,128)(2,1)}, u32[]{:S(2)}) copy-start(bf16[6144,256]{1,0:T(8,128)(2,1)} %param.17) | copy-start | bytes 9437188
  6.5 4.1 %copy-start.3 = (bf16[1,32,6144]{2,1,0:T(8,128)(2,1)S(1)}, bf16[1,32,6144]{2,1,0:T(8,128)(2,1)}, u32[]{:S(2)}) copy-start(bf16[1,32,6144]{2,1,0:T(8,128)(2,1)} %param.11) | copy-start | bytes 1179652
  6.5 121.9 %all-gather.3.cloned.1.call-start = ((), (), s32[]{:S(2)}) async-start(), calls=%async_computation.1 | async-start | bytes 6684672 | tf_op jit(solution)/shard_map/all_gather | solution.py:32
  11.6 178.3 %all-gather.5.cloned.1.call-start = ((), (), s32[]{:S(2)}) async-start(), calls=%async_computation.2 | async-start | bytes 8912896 | tf_op jit(solution)/shard_map/all_gather | solution.py:16
  128.4 4.8 %copy-start.5 = (bf16[512,6144]{1,0:T(8,128)(2,1)S(1)}, bf16[512,6144]{1,0:T(8,128)(2,1)}, u32[]{:S(2)}) copy-start(bf16[512,6144]{1,0:T(8,128)(2,1)} %all-gather.3.cloned.1.call-done) | copy-start | bytes 18874372
  128.4 5.5 %copy-start.6 = (bf16[6144,256]{1,0:T(8,128)(2,1)S(1)}, bf16[6144,256]{1,0:T(8,128)(2,1)}, u32[]{:S(2)}) copy-start(bf16[6144,256]{1,0:T(8,128)(2,1)} %param.16) | copy-start | bytes 9437188
  144.0 52.6 %copy-start.4 = (s32[512]{0:T(512)S(1)}, s32[512]{0:T(512)}, u32[]{:S(2)}) copy-start(s32[512]{0:T(512)} %param.13) | copy-start | bytes 6148
  196.9 2.4 copy-start.1
  200.3 0.8 copy-start.2
  201.4 2.4 copy-start.1
  204.9 0.8 copy-start.2
  206.0 2.4 copy-start.1
  209.4 0.8 copy-start.2
  210.5 2.4 copy-start.1
  214.0 0.8 copy-start.2
  215.1 2.4 copy-start.1
  218.5 0.8 copy-start.2
  219.6 2.4 copy-start.1
  223.0 0.8 copy-start.2
  224.1 2.4 copy-start.1
  227.6 0.8 copy-start.2
  228.7 2.4 copy-start.1
  232.1 0.8 copy-start.2
  233.2 2.4 copy-start.1
  237.8 2.4 copy-start.1
  242.3 2.4 copy-start.1
  246.8 2.4 copy-start.1
  251.4 2.4 copy-start.1
  255.9 2.4 copy-start.1
  260.5 2.4 copy-start.1
  265.0 2.4 copy-start.1
  268.4 0.8 copy-start.2
  (7 other events, 5.6 us)
Sparse Core Ops, SparseCore 0:
  11.8 116.6 all-gather.2
  136.8 53.1 all-gather.4
where the time goes:
time: 298 us; the launch traced here: 297 us
  waiting for transfers between devices  163 us (55%)
  local copies, waits for them, and re-layouts  43.1 us (14%)
  matrix products  40.3 us (14%)
  blocking collectives  17.8 us (6%)
  other arithmetic  17.2 us (6%)
  between operations  14.3 us (5%)
    all_gather x1, waiting for transfers between devices, per_device(): piece = lax.all_gather(modulated, 'dp', axis=0, tiled=True)  117 us
    all_gather x1, waiting for transfers between devices, in_one_piece(): lax.all_gather(both, axis, axis=dim, tiled=True)  45.9 us
    dynamic_slice x16, local copies, waits for them, and re-layouts, single(): value_block = lax.dynamic_slice_in_dim(piece[1], index * tokc, tokc, 0)  18.1 us
    all_to_all x1, blocking collectives, per_device(): lax.all_to_all(result, 'dp', split_axis=0, concat_axis=1, tiled=True)  17.8 us
    dot_general x16, matrix products, update(): jnp.einsum('htk,khd->thd', weights.astype(jnp.bfloat16), value_block.resh...  17 us
    cond x80, local copies, waits for them, and re-layouts  12.7 us
    dot_general x16, matrix products, update(): jnp.einsum('thd,khd->htk', query, key_block.reshape(tokc, HEAD_DEV, HD),...  10.1 us
    reduce_sum x16, other arithmetic, update(): total = total * fade + jnp.sum(weights, axis=-1)  9.03 us
  transfers between devices with their start and end apart: 2, of which 2 were waited for; matrix products, arithmetic and copies ran while one was open for 2% of the time, Pallas kernels for 0%

commit v1 on v0

v1 whole, which is shorter than its diff:
```python
import math

import jax
import jax.numpy as jnp
from jax import lax
from jax.experimental import pallas as pl
from jax.experimental.pallas import tpu as pltpu
from jax.sharding import PartitionSpec as P

D = 6144
HD = 128
HALF = D // 2
MESH = pl.DeviceIdType.MESH
NEG = -1e30
BF = jnp.bfloat16
F32 = jnp.float32


def kernel(
    lat, steps, seg, mod, wq, wk, wv, out,
    x_buf, w_buf, mod_all, mod_row, xn, q_own, kv_own, q_in, kv_in, s_buf, bias, seg_buf, o_buf, o_in,
    xs, xr, ls, es, er, os_, or_,
):
    g = lax.axis_index("group")
    d = lax.axis_index("dp")
    xh = d // 8
    z = d % 8
    head = g // 8
    win = g % 8

    def at_z(k):
        return {"group": g, "dp": xh * 8 + (z + k + 8) % 8}

    across = {"group": g, "dp": (d + 8) % 16}
    up, down = at_z(1), at_z(-1)

    barrier = pltpu.get_barrier_semaphore()
    for peer in (up, down, across):
        pl.semaphore_signal(barrier, inc=1, device_id=peer, device_id_type=MESH)
    for k in range(1, 16):
        pl.semaphore_signal(barrier, inc=1, device_id={"group": (g + k) % 16, "dp": d}, device_id_type=MESH)

    def own_slot(half):
        return 2 * d + half

    def other(k, half):
        return 2 * ((1 - xh) * 8 + (z + k + 8) % 8) + half

    def same(k, half):
        return 2 * (xh * 8 + (z + k + 8) % 8) + half

    loads = [
        pltpu.make_async_copy(lat.at[0, pl.ds(0, 16)], x_buf.at[own_slot(0)], ls.at[0]),
        pltpu.make_async_copy(lat.at[0, pl.ds(16, 16)], x_buf.at[own_slot(1)], ls.at[1]),
        pltpu.make_async_copy(mod, mod_all, ls.at[2]),
        pltpu.make_async_copy(seg, seg_buf, ls.at[3]),
        pltpu.make_async_copy(wq, w_buf.at[0], ls.at[4]),
        pltpu.make_async_copy(wk, w_buf.at[1], ls.at[5]),
        pltpu.make_async_copy(wv, w_buf.at[2], ls.at[6]),
    ]
    for c in loads:
        c.start()
    pl.semaphore_wait(barrier, 18)

    sends = []

    def send(src, dst, to, recv):
        c = pltpu.make_async_remote_copy(
            src_ref=src, dst_ref=dst, send_sem=xs.at[len(sends)], recv_sem=recv, device_id=to, device_id_type=MESH
        )
        c.start()
        sends.append(c)

    def send_own(half, to):
        send(lat.at[0, pl.ds(16 * half, 16)], x_buf.at[own_slot(half)], to, xr.at[own_slot(half)])

    def relay(slot, to):
        send(x_buf.at[slot], x_buf.at[slot], to, xr.at[slot])

    def relay_half(slot, part, to):
        cols = pl.ds(part * HALF, HALF)
        sem = xr.at[slot] if part == 0 else xr.at[32]
        send(x_buf.at[slot, :, cols], x_buf.at[slot, :, cols], to, sem)

    def arrived(slot):
        pltpu.make_async_remote_copy(
            src_ref=x_buf.at[slot], dst_ref=x_buf.at[slot], send_sem=xs.at[0], recv_sem=xr.at[slot],
            device_id=up, device_id_type=MESH,
        ).wait_recv()

    def arrived_half(slot, part):
        cols = pl.ds(part * HALF, HALF)
        sem = xr.at[slot] if part == 0 else xr.at[32]
        pltpu.make_async_remote_copy(
            src_ref=x_buf.at[slot, :, cols], dst_ref=x_buf.at[slot, :, cols], send_sem=xs.at[0], recv_sem=sem,
            device_id=up, device_id_type=MESH,
        ).wait_recv()

    send_own(0, up)
    send_own(0, down)
    send_own(0, across)
    send_own(1, up)
    send_own(1, down)
    send_own(1, across)

    loads[2].wait()
    row = mod_all[steps[0]]
    mod_row[0:1, :] = 1.0 + row[0:1, :]
    mod_row[1:2, :] = row[1:2, :]
    loads[3].wait()
    for w in range(8):
        first = min(max(64 * w - 64, 0), 320)

        @pl.when(win == w)
        def _(w=w, first=first):
            sq = jnp.broadcast_to(seg_buf[0:1, 64 * w : 64 * w + 64], (64, 64))
            diag = lax.broadcasted_iota(jnp.int32, (64, 64), 0) == lax.broadcasted_iota(jnp.int32, (64, 64), 1)
            col = jnp.sum(jnp.where(diag, sq, 0.0), axis=1, keepdims=True)
            sk = seg_buf[0:1, first : first + 192]
            tile = jnp.where(col == sk, 0.0, NEG)
            wide = jnp.concatenate([tile] * 4, axis=1)
            for i in range(4):
                bias[0, 64 * i : 64 * i + 64, :] = wide
                parts = [tile if j <= i else jnp.full((64, 192), NEG, F32) for j in range(4)]
                bias[1, 64 * i : 64 * i + 64, :] = jnp.concatenate(parts, axis=1)

    def norm(slot, at):
        x = x_buf[slot].astype(F32)
        inv = lax.rsqrt(jnp.mean(x * x, axis=-1, keepdims=True) + 1e-06)
        xn[pl.ds(16 * at, 16), :] = (x * inv * mod_row[0:1, :] + mod_row[1:2, :]).astype(BF)

    def project(which, slots):
        n = 16 * len(slots)
        r = jnp.dot(xn[0:n, :], w_buf[which], preferred_element_type=F32).astype(BF)
        for i, slot in enumerate(slots):
            for h in range(2):
                piece = r[16 * i : 16 * i + 16, HD * h : HD * h + HD]
                if which == 0:
                    q_own[h, slot] = piece
                else:
                    kv_own[h, slot, :, HD * (which - 1) : HD * which] = piece

    loads[0].wait()
    loads[1].wait()
    norm(own_slot(0), 0)
    norm(own_slot(1), 1)

    arrived(other(0, 0))
    relay(other(0, 0), up)
    relay(other(0, 0), down)
    chunk = [own_slot(0), own_slot(1), other(0, 0), other(0, 1)]

    for s in range(1, 4):
        a, b = same(-s, 0), same(s, 0)
        arrived(a)
        relay(a, up)
        arrived(b)
        if s < 3:
            relay(b, down)
        if s == 1:
            norm(chunk[2], 2)
        else:
            for i in range(4):
                norm(chunk[i], i)
        a, b = same(-s, 1), same(s, 1)
        arrived(a)
        if s < 3:
            relay(a, up)
        relay(a, across)
        arrived(b)
        relay(b, down)
        relay(b, across)
        if s == 1:
            arrived(chunk[3])
            norm(chunk[3], 3)
            for i in (4, 5, 6):
                loads[i].wait()
        else:
            norm(chunk[4], 4)
            norm(chunk[5], 5)
        a, b = other(-s, 0), other(s, 0)
        arrived(a)
        if s < 3:
            relay(a, up)
        else:
            relay_half(a, 0, up)
        arrived(b)
        if s < 3:
            relay(b, down)
        else:
            relay_half(b, 1, down)
        if s > 1:
            for i in (6, 7):
                arrived(chunk[i])
                norm(chunk[i], i)
        for which in range(3):
            project(which, chunk)
        chunk = [same(-s, 0), same(s, 0), same(-s, 1), same(s, 1), other(-s, 0), other(s, 0), other(-s, 1), other(s, 1)]

    for i in range(4):
        norm(chunk[i], i)
    arrived(same(4, 1))
    relay(same(4, 1), across)
    arrived(same(4, 0))
    norm(chunk[4], 4)
    norm(chunk[5], 5)
    for i in (6, 7):
        arrived(chunk[i])
        norm(chunk[i], i)
    for which in range(3):
        project(which, chunk)
    chunk = [same(4, 0), same(4, 1), other(4, 0), other(4, 1)]
    norm(chunk[0], 0)
    norm(chunk[1], 1)
    arrived_half(chunk[2], 0)
    arrived_half(chunk[2], 1)
    norm(chunk[2], 2)
    arrived(chunk[3])
    norm(chunk[3], 3)
    for which in range(3):
        project(which, chunk)

    ex = []
    for k in range(1, 16):
        t = (g + k) % 16
        th, tw = t // 8, t % 8
        first = jnp.minimum(jnp.maximum(4 * tw - 4, 0), 20)
        to = {"group": t, "dp": d}
        ex.append(
            pltpu.make_async_remote_copy(
                src_ref=kv_own.at[th, pl.ds(first, 12)], dst_ref=kv_in.at[g], send_sem=es.at[0, k],
                recv_sem=er.at[0, g], device_id=to, device_id_type=MESH,
            )
        )
        ex.append(
            pltpu.make_async_remote_copy(
                src_ref=q_own.at[th, pl.ds(4 * tw, 4)], dst_ref=q_in.at[g], send_sem=es.at[1, k],
                recv_sem=er.at[1, g], device_id=to, device_id_type=MESH,
            )
        )
    for c in ex:
        c.start()
    first = jnp.minimum(jnp.maximum(4 * win - 4, 0), 20)
    mine = [
        pltpu.make_async_copy(kv_own.at[head, pl.ds(first, 12)], kv_in.at[g], ls.at[7]),
        pltpu.make_async_copy(q_own.at[head, pl.ds(4 * win, 4)], q_in.at[g], ls.at[8]),
    ]
    for c in mine:
        c.start()
    for c in mine:
        c.wait()
    for k in range(1, 16):
        t = (g + k) % 16
        for i, (own, land) in enumerate(((kv_own.at[0, pl.ds(0, 12)], kv_in.at[t]), (q_own.at[0, pl.ds(0, 4)], q_in.at[t]))):
            pltpu.make_async_remote_copy(
                src_ref=own, dst_ref=land, send_sem=es.at[i, k], recv_sem=er.at[i, t], device_id=up, device_id_type=MESH
            ).wait_recv()

    scale = 1.0 / math.sqrt(HD)
    outs = []
    for b in range(4):
        q = q_in[4 * b : 4 * b + 4].reshape(256, HD)
        best = jnp.full((256, 1), NEG, F32)
        for kb in range(b + 1):
            keys = kv_in[4 * kb : 4 * kb + 4, :, :, 0:HD].reshape(768, HD)
            sc = lax.dot_general(q, keys, (((1,), (1,)), ((), ())), preferred_element_type=F32)
            sc = sc * scale + bias[1 if kb == b else 0]
            s_buf[:, 768 * kb : 768 * kb + 768] = sc
            best = jnp.maximum(best, jnp.max(sc, axis=-1, keepdims=True))
        total = jnp.zeros((256, 1), F32)
        acc = jnp.zeros((256, HD), F32)
        for kb in range(b + 1):
            p = jnp.exp(s_buf[:, 768 * kb : 768 * kb + 768] - best)
            total = total + jnp.sum(p, axis=-1, keepdims=True)
            vals = kv_in[4 * kb : 4 * kb + 4, :, :, HD : 2 * HD].reshape(768, HD)
            acc = acc + jnp.dot(p.astype(BF), vals, preferred_element_type=F32)
        o_buf[4 * b : 4 * b + 4] = (acc / total).astype(BF).reshape(4, 4, 16, HD)

    col = pl.multiple_of((2 * d + head) * HD, HD)
    cols = pl.ds(col, HD)
    for half in range(2):
        td = 2 * win + half
        for c in range(16):
            src = o_buf.at[c, pl.ds(2 * half, 2)]
            dst = o_in.at[:, :, cols]
            away = jnp.logical_or(g != c, d != td)
            rc = pltpu.make_async_remote_copy(
                src_ref=src, dst_ref=dst, send_sem=os_.at[half, c], recv_sem=or_.at[2 * d + head],
                device_id={"group": c, "dp": td}, device_id_type=MESH,
            )
            lc = pltpu.make_async_copy(src, dst, ls.at[9])

            @pl.when(away)
            def _(rc=rc):
                rc.start()

            @pl.when(jnp.logical_not(away))
            def _(lc=lc):
                lc.start()
                lc.wait()

    for hd in range(32):
        src_g = (hd % 2) * 8 + d // 2
        here = jnp.logical_and(src_g == g, hd // 2 == d)

        @pl.when(jnp.logical_not(here))
        def _(hd=hd):
            pltpu.make_async_remote_copy(
                src_ref=o_buf.at[0, pl.ds(0, 2)], dst_ref=o_in.at[:, :, pl.ds(hd * HD, HD)], send_sem=os_.at[0, 0],
                recv_sem=or_.at[hd], device_id=up, device_id_type=MESH,
            ).wait_recv()

    final = pltpu.make_async_copy(o_in, out, ls.at[10])
    final.start()

    for c in sends:
        c.wait_send()
    for c in ex:
        c.wait_send()
    for half in range(2):
        td = 2 * win + half
        for c in range(16):
            away = jnp.logical_or(g != c, d != td)

            @pl.when(away)
            def _(half=half, c=c):
                pltpu.make_async_remote_copy(
                    src_ref=o_buf.at[c, pl.ds(2 * half, 2)], dst_ref=o_in.at[:, :, pl.ds(0, HD)], send_sem=os_.at[half, c],
                    recv_sem=or_.at[0], device_id=up, device_id_type=MESH,
                ).wait_send()
    final.wait()


def per_device(latents, steps, segment_ids, mod_table, w_query, w_key, w_value):
    anywhere = pl.BlockSpec(memory_space=pl.ANY)
    vmem = pltpu.VMEM
    dma = pltpu.SemaphoreType.DMA
    out = pl.pallas_call(
        kernel,
        out_shape=jax.ShapeDtypeStruct((2, 16, 4096), BF),
        in_specs=[anywhere, pl.BlockSpec(memory_space=pltpu.SMEM)] + [anywhere] * 5,
        out_specs=anywhere,
        scratch_shapes=[
            vmem((32, 16, D), BF),
            vmem((3, D, 256), BF),
            vmem((16, 2, D), F32),
            vmem((2, D), F32),
            vmem((128, D), BF),
            vmem((2, 32, 16, HD), BF),
            vmem((2, 32, 16, 2 * HD), BF),
            vmem((16, 4, 16, HD), BF),
            vmem((16, 12, 16, 2 * HD), BF),
            vmem((256, 3072), F32),
            vmem((2, 256, 768), F32),
            vmem((1, 512), F32),
            vmem((16, 4, 16, HD), BF),
            vmem((2, 16, 4096), BF),
            dma((48,)),
            dma((33,)),
            dma((11,)),
            dma((2, 16)),
            dma((2, 16)),
            dma((2, 16)),
            dma((32,)),
        ],
        name="block",
        compiler_params=pltpu.CompilerParams(
            collective_id=0, has_side_effects=True, vmem_limit_bytes=58 * 1024 * 1024
        ),
    )(latents, steps, segment_ids.astype(F32).reshape(1, 512), mod_table, w_query, w_key, w_value)
    return out.reshape(1, 32, 4096)


def solution(mesh):
    placed = (
        P("group", "dp", None),
        P("group"),
        P(),
        P(),
        P(None, "dp"),
        P(None, "dp"),
        P(None, "dp"),
    )
    return jax.shard_map(
        per_device, mesh=mesh, in_specs=placed, out_specs=P("group", "dp", None), check_vma=False
    )
```

time: 298 us -> 109 us (0.37)
  the two profiles are of different devices: /device:TPU:27 before, /device:TPU:39 now
where the time goes in v1:
time: 109 us
  Pallas kernels  105 us (96%)
  local copies, waits for them, and re-layouts  1.67 us (2%)
  other arithmetic  1.26 us (1%)
    pallas_call x1, Pallas kernels, per_device(): pl.pallas_call(kernel, out_shape=jax.ShapeDtypeStruct((2, 16, 4096), BF),...  105 us

profile of v1, /device:TPU:39, one launch (start us, length us, event | category | flops | bytes accessed | tf_op | source)
XLA Modules:
  0.0 108.9 jit_solution(5990028292992950065)
XLA Ops:
  0.7 1.3 %convert_element_type.3 = f32[512]{0:T(512)} convert(s32[512]{0:T(512)} %param.9) | non-fusion elementwise | flops 512 | bytes 4096 | tf_op jit(solution)/shard_map/convert_element_type | solution.py:370
  1.9 105.3 %block.1 = bf16[2,16,4096]{2,1,0:T(8,128)(2,1)} custom-call(bf16[1,32,6144]{2,1,0:T(8,128)(2,1)} %lat.1, s32[1]{0:T(128)S(6)} %copy.9.steps, f32[1,512]{1,0:T(1,128)} %bitcast.3, f32[16,2,6144]{2,1,0:T(2,128)} %mod.1, bf16[6144,256]{1,0:T(8,128)(2,1)} %wq.1, bf16[6144,256]{1,0:T(8,128)(2,1)} %wk.1, bf16[6144,256]{1,0:T(8,128)(2,1)} %wv.1), custom_call_target="tpu_custom_call" | custom-call | tf_op jit(solution)/shard_map/block/pallas_call | solution.py:338
  107.2 1.7 %copy.10 = bf16[1,32,4096]{2,1,0:T(8,128)(2,1)} copy(bf16[1,32,4096]{2,1,0:T(8,128)(2,1)} %bitcast.2) | data formatting | bytes 524288

commit v2 on v1

v2 whole, which is shorter than its diff:
```python
import math

import jax
import jax.numpy as jnp
from jax import lax
from jax.experimental import pallas as pl
from jax.experimental.pallas import tpu as pltpu
from jax.sharding import PartitionSpec as P

D = 6144
HD = 128
HALF = D // 2
MESH = pl.DeviceIdType.MESH
NEG = -1e30
BF = jnp.bfloat16
F32 = jnp.float32


def kernel(
    lat, steps, seg, mod, wq, wk, wv, out,
    x_buf, w_buf, mod_all, mod_row, xn, own, partner, q_in, kv_in, s_buf, bias, seg_buf, o_buf, o_in,
    xs, xr, ls, ps, pr, es, er, lx, os_, or_,
):
    g = lax.axis_index("group")
    d = lax.axis_index("dp")
    xh = d // 8
    z = d % 8
    head = g // 8
    mate = (g + 8) % 16
    win = (g % 8 + 2 * z) % 8

    def at_z(k):
        return {"group": g, "dp": xh * 8 + (z + k + 8) % 8}

    across = {"group": g, "dp": (d + 8) % 16}
    up, down = at_z(1), at_z(-1)

    barrier = pltpu.get_barrier_semaphore()
    for peer in (up, down, across):
        pl.semaphore_signal(barrier, inc=1, device_id=peer, device_id_type=MESH)
    for k in range(1, 8):
        pl.semaphore_signal(
            barrier, inc=1, device_id={"group": head * 8 + (g + k) % 8, "dp": d}, device_id_type=MESH
        )
    pl.semaphore_signal(barrier, inc=1, device_id={"group": mate, "dp": d}, device_id_type=MESH)

    def block_same(k):
        return xh * 8 + (z + k + 8) % 8

    def block_other(k):
        return (1 - xh) * 8 + (z + k + 8) % 8

    def same(k, half):
        return 2 * block_same(k) + half

    def other(k, half):
        return 2 * block_other(k) + half

    loads = [
        pltpu.make_async_copy(lat.at[0, pl.ds(0, 16)], x_buf.at[same(0, 0)], ls.at[0]),
        pltpu.make_async_copy(lat.at[0, pl.ds(16, 16)], x_buf.at[same(0, 1)], ls.at[1]),
        pltpu.make_async_copy(mod, mod_all, ls.at[2]),
        pltpu.make_async_copy(seg, seg_buf, ls.at[3]),
        pltpu.make_async_copy(wq, w_buf.at[0], ls.at[4]),
        pltpu.make_async_copy(wk, w_buf.at[1], ls.at[5]),
        pltpu.make_async_copy(wv, w_buf.at[2], ls.at[6]),
    ]
    for c in loads:
        c.start()
    pl.semaphore_wait(barrier, 11)

    sends = []

    def send(src, dst, to, recv):
        c = pltpu.make_async_remote_copy(
            src_ref=src, dst_ref=dst, send_sem=xs.at[len(sends)], recv_sem=recv, device_id=to, device_id_type=MESH
        )
        c.start()
        sends.append(c)

    def send_own(half, to):
        send(lat.at[0, pl.ds(16 * half, 16)], x_buf.at[same(0, half)], to, xr.at[same(0, half)])

    def relay(slot, to):
        send(x_buf.at[slot], x_buf.at[slot], to, xr.at[slot])

    def relay_half(slot, part, to):
        cols = pl.ds(part * HALF, HALF)
        sem = xr.at[slot] if part == 0 else xr.at[32]
        send(x_buf.at[slot, :, cols], x_buf.at[slot, :, cols], to, sem)

    def arrived(slot):
        pltpu.make_async_remote_copy(
            src_ref=x_buf.at[slot], dst_ref=x_buf.at[slot], send_sem=xs.at[0], recv_sem=xr.at[slot],
            device_id=up, device_id_type=MESH,
        ).wait_recv()

    def arrived_half(slot, part):
        cols = pl.ds(part * HALF, HALF)
        sem = xr.at[slot] if part == 0 else xr.at[32]
        pltpu.make_async_remote_copy(
            src_ref=x_buf.at[slot, :, cols], dst_ref=x_buf.at[slot, :, cols], send_sem=xs.at[0], recv_sem=sem,
            device_id=up, device_id_type=MESH,
        ).wait_recv()

    send_own(0, across)
    send_own(0, up)
    send_own(0, down)
    send_own(1, up)
    send_own(1, down)
    send_own(1, across)

    loads[2].wait()
    row = mod_all[steps[0]]
    mod_row[0:1, :] = 1.0 + row[0:1, :]
    mod_row[1:2, :] = row[1:2, :]
    loads[3].wait()
    for w in range(8):
        first = min(max(64 * w - 64, 0), 320)

        @pl.when(win == w)
        def _(w=w, first=first):
            sq = jnp.broadcast_to(seg_buf[0:1, 64 * w : 64 * w + 64].astype(F32), (64, 64))
            diag = lax.broadcasted_iota(jnp.int32, (64, 64), 0) == lax.broadcasted_iota(jnp.int32, (64, 64), 1)
            col = jnp.sum(jnp.where(diag, sq, 0.0), axis=1, keepdims=True)
            sk = seg_buf[0:1, first : first + 192].astype(F32)
            tile = jnp.where(col == sk, 0.0, NEG)
            wide = jnp.concatenate([tile] * 4, axis=1)
            for i in range(4):
                bias[0, 64 * i : 64 * i + 64, :] = wide
                parts = [tile if j <= i else jnp.full((64, 192), NEG, F32) for j in range(4)]
                bias[1, 64 * i : 64 * i + 64, :] = jnp.concatenate(parts, axis=1)

    def norm(slot, at):
        x = x_buf[slot].astype(F32)
        inv = lax.rsqrt(jnp.mean(x * x, axis=-1, keepdims=True) + 1e-06)
        xn[pl.ds(16 * at, 16), :] = (x * inv * mod_row[0:1, :] + mod_row[1:2, :]).astype(BF)

    def project(which, slots):
        n = 16 * len(slots)
        r = jnp.dot(xn[0:n, :], w_buf[which], preferred_element_type=F32).astype(BF)
        for i, slot in enumerate(slots):
            for h in range(2):
                own[h, slot, :, HD * which : HD * which + HD] = r[16 * i : 16 * i + 16, HD * h : HD * h + HD]

    def swap(block):
        two = pl.ds(2 * block, 2)
        return pltpu.make_async_remote_copy(
            src_ref=own.at[1 - head, two], dst_ref=partner.at[two], send_sem=ps.at[block], recv_sem=pr.at[block],
            device_id={"group": mate, "dp": d}, device_id_type=MESH,
        )

    def spread(block, whose):
        src = own.at[head] if whose == 0 else partner
        c = g if whose == 0 else mate
        two = pl.ds(2 * block, 2)
        mid = block // 2

        def to_window(i, carry):
            w = mid + i - 2
            cw = jnp.minimum(jnp.maximum(w, 1), 6)
            near = jnp.logical_and(mid - cw <= 1, cw - mid <= 1)
            use = jnp.logical_and(near, jnp.logical_and(w >= 0, w <= 7))
            place = (w + 16 - 2 * z) % 8
            here = place == g % 8
            to = {"group": head * 8 + place, "dp": d}
            rest = pl.ds(2 * block - 4 * (cw - 1), 2)
            kv_src, kv_dst = src.at[two, :, pl.ds(HD, 2 * HD)], kv_in.at[c, rest]
            q_src, q_dst = src.at[two, :, pl.ds(0, HD)], q_in.at[c, pl.ds(2 * (block % 2), 2)]

            @pl.when(jnp.logical_and(use, jnp.logical_not(here)))
            def _():
                pltpu.make_async_remote_copy(
                    src_ref=kv_src, dst_ref=kv_dst, send_sem=es.at[0, whose, place], recv_sem=er.at[0, c],
                    device_id=to, device_id_type=MESH,
                ).start()

            @pl.when(jnp.logical_and(use, here))
            def _():
                pltpu.make_async_copy(kv_src, kv_dst, lx.at[0, whose]).start()

            @pl.when(jnp.logical_and(i == 2, jnp.logical_not(here)))
            def _():
                pltpu.make_async_remote_copy(
                    src_ref=q_src, dst_ref=q_dst, send_sem=es.at[1, whose, place], recv_sem=er.at[1, c],
                    device_id=to, device_id_type=MESH,
                ).start()

            @pl.when(jnp.logical_and(i == 2, here))
            def _():
                pltpu.make_async_copy(q_src, q_dst, lx.at[1, whose]).start()

            return carry

        lax.fori_loop(0, 5, to_window, 0)

    todo = []

    def work(budget):
        while todo and budget > 0:
            cost, call = todo.pop(0)
            call()
            budget -= cost

    def norms(slots, at, wait):
        def call():
            for i in at:
                if wait:
                    arrived(slots[i])
                norm(slots[i], i)
        return call

    def plan(slots, blocks, before):
        n = len(slots)
        for at in range(0, n, 2):
            todo.append((0.5 if at < 4 else 1.0, norms(slots, (at, at + 1), at == 6)))
        for which in range(3):
            todo.append((1.0, lambda which=which: project(which, slots)))

        def out_own():
            for b in blocks:
                swap(b).start()
            for b in blocks:
                spread(b, 0)

        todo.append((1.0, out_own))
        if before:
            todo.append((0.5, lambda: out_mate(before)))

    def out_mate(blocks):
        for b in blocks:
            swap(b).wait_recv()
        for b in blocks:
            spread(b, 1)

    arrived(other(0, 0))
    relay(other(0, 0), up)
    relay(other(0, 0), down)
    loads[0].wait()
    loads[1].wait()
    slots = [same(0, 0), same(0, 1), other(0, 0), other(0, 1)]
    blocks = [block_same(0), block_other(0)]
    todo.append((0.5, norms(slots, (0, 1), False)))
    todo.append((0.5, norms(slots, (2,), False)))

    def ready():
        for i in (4, 5, 6):
            loads[i].wait()
        arrived(slots[3])
        norm(slots[3], 3)

    todo.append((0.5, lambda ready=ready: ready()))
    for which in range(3):
        todo.append((1.0, lambda which=which, slots=slots: project(which, slots)))

    def first_out(blocks=blocks):
        for b in blocks:
            swap(b).start()
        for b in blocks:
            spread(b, 0)

    todo.append((1.0, first_out))

    before = blocks
    for s in range(1, 4):
        for half in range(2):
            a, b = same(-s, half), same(s, half)
            arrived(a)
            if s < 3 or half == 0:
                relay(a, up)
            if half == 1:
                relay(a, across)
            work(1.0)
            arrived(b)
            if s < 3 or half == 1:
                relay(b, down)
            if half == 1:
                relay(b, across)
            work(1.0)
        a, b = other(-s, 0), other(s, 0)
        arrived(a)
        if s < 3:
            relay(a, up)
        else:
            relay_half(a, 0, up)
        work(1.0)
        arrived(b)
        if s < 3:
            relay(b, down)
        else:
            relay_half(b, 1, down)
        work(1.0)
        chunk = [same(-s, 0), same(s, 0), same(-s, 1), same(s, 1), other(-s, 0), other(s, 0), other(-s, 1), other(s, 1)]
        blocks = [block_same(-s), block_same(s), block_other(-s), block_other(s)]
        plan(chunk, blocks, before)
        before = blocks

    work(1.0)
    arrived(same(4, 1))
    relay(same(4, 1), across)
    work(100.0)
    chunk = [same(4, 0), same(4, 1), other(4, 0), other(4, 1)]
    blocks = [block_same(4), block_other(4)]
    arrived(chunk[0])
    norm(chunk[0], 0)
    norm(chunk[1], 1)
    out_mate(before)
    arrived_half(chunk[2], 0)
    arrived_half(chunk[2], 1)
    norm(chunk[2], 2)
    arrived(chunk[3])
    norm(chunk[3], 3)
    for which in range(3):
        project(which, chunk)
    for b in blocks:
        swap(b).start()
    for b in blocks:
        spread(b, 0)
    out_mate(blocks)

    kv_whole, q_whole = own.at[0, pl.ds(0, 12), :, pl.ds(HD, 2 * HD)], own.at[0, pl.ds(0, 4), :, pl.ds(0, HD)]

    def whole(i, whose, place, c):
        return pltpu.make_async_remote_copy(
            src_ref=(kv_whole, q_whole)[i], dst_ref=(kv_in, q_in)[i].at[c], send_sem=es.at[i, whose, place],
            recv_sem=er.at[i, c], device_id=up, device_id_type=MESH,
        )

    for whose in range(2):
        c = (g, mate)[whose]
        pltpu.make_async_copy(kv_whole, kv_in.at[c], lx.at[0, whose]).wait()
        pltpu.make_async_copy(q_whole, q_in.at[c], lx.at[1, whose]).wait()
    for k in range(1, 8):
        c = (g + k) % 8
        for side in range(2):
            for i in range(2):
                whole(i, 0, 0, c + 8 * side).wait_recv()

    scale = 1.0 / math.sqrt(HD)

    def attend(b):
        q = q_in[4 * b : 4 * b + 4].reshape(256, HD)
        best = jnp.full((256, 1), NEG, F32)
        for kb in range(b + 1):
            keys = kv_in[4 * kb : 4 * kb + 4, :, :, 0:HD].reshape(768, HD)
            sc = lax.dot_general(q, keys, (((1,), (1,)), ((), ())), preferred_element_type=F32)
            sc = sc * scale + bias[1 if kb == b else 0]
            s_buf[:, 768 * kb : 768 * kb + 768] = sc
            best = jnp.maximum(best, jnp.max(sc, axis=-1, keepdims=True))
        total = jnp.zeros((256, 1), F32)
        acc = jnp.zeros((256, HD), F32)
        for kb in range(b + 1):
            p = jnp.exp(s_buf[:, 768 * kb : 768 * kb + 768] - best)
            total = total + jnp.sum(p, axis=-1, keepdims=True)
            vals = kv_in[4 * kb : 4 * kb + 4, :, :, HD : 2 * HD].reshape(768, HD)
            acc = acc + jnp.dot(p.astype(BF), vals, preferred_element_type=F32)
        o_buf[4 * b : 4 * b + 4] = (acc / total).astype(BF).reshape(4, 4, 16, HD)

    cols = pl.ds(pl.multiple_of((2 * d + head) * HD, HD), HD)

    def home(c, half):
        return pltpu.make_async_remote_copy(
            src_ref=o_buf.at[c, pl.ds(2 * half, 2)], dst_ref=o_in.at[:, :, cols], send_sem=os_.at[half, c],
            recv_sem=or_.at[2 * d + head], device_id={"group": c, "dp": 2 * win + half}, device_id_type=MESH,
        )

    def away(c, half):
        return jnp.logical_or(g != c, d != 2 * win + half)

    def send_home(b):
        for c in range(4 * b, 4 * b + 4):
            for half in range(2):
                far = away(c, half)

                @pl.when(far)
                def _(c=c, half=half):
                    home(c, half).start()

                @pl.when(jnp.logical_not(far))
                def _(c=c, half=half):
                    lc = pltpu.make_async_copy(o_buf.at[c, pl.ds(2 * half, 2)], o_in.at[:, :, cols], ls.at[7])
                    lc.start()
                    lc.wait()

    attend(3)
    for b in (2, 1, 0):
        attend(b)
        send_home(b + 1)
    send_home(0)

    for hd in range(32):
        src_d = hd // 2
        src_g = (hd % 2) * 8 + (d // 2 + 16 - 2 * (src_d % 8)) % 8
        remote = jnp.logical_or(src_g != g, src_d != d)

        @pl.when(remote)
        def _(hd=hd):
            pltpu.make_async_remote_copy(
                src_ref=o_buf.at[0, pl.ds(0, 2)], dst_ref=o_in.at[:, :, pl.ds(hd * HD, HD)], send_sem=os_.at[0, 0],
                recv_sem=or_.at[hd], device_id=up, device_id_type=MESH,
            ).wait_recv()

    final = pltpu.make_async_copy(o_in, out, ls.at[8])
    final.start()

    for c in sends:
        c.wait_send()
    for b in range(16):
        swap(b).wait_send()
    for k in range(1, 8):
        w = (g + k) % 8
        for whose in range(2):
            for i in range(2):
                whole(i, whose, w, 0).wait_send()
    for half in range(2):
        for c in range(16):
            @pl.when(away(c, half))
            def _(half=half, c=c):
                home(c, half).wait_send()
    final.wait()


def per_device(latents, steps, segment_ids, mod_table, w_query, w_key, w_value):
    anywhere = pl.BlockSpec(memory_space=pl.ANY)
    vmem = pltpu.VMEM
    dma = pltpu.SemaphoreType.DMA
    out = pl.pallas_call(
        kernel,
        out_shape=jax.ShapeDtypeStruct((2, 16, 4096), BF),
        in_specs=[anywhere, pl.BlockSpec(memory_space=pltpu.SMEM)] + [anywhere] * 5,
        out_specs=anywhere,
        scratch_shapes=[
            vmem((32, 16, D), BF),
            vmem((3, D, 256), BF),
            vmem((16, 2, D), F32),
            vmem((2, D), F32),
            vmem((128, D), BF),
            vmem((2, 32, 16, 3 * HD), BF),
            vmem((32, 16, 3 * HD), BF),
            vmem((16, 4, 16, HD), BF),
            vmem((16, 12, 16, 2 * HD), BF),
            vmem((256, 3072), F32),
            vmem((2, 256, 768), F32),
            vmem((1, 512), jnp.int32),
            vmem((16, 4, 16, HD), BF),
            vmem((2, 16, 4096), BF),
            dma((48,)),
            dma((33,)),
            dma((9,)),
            dma((16,)),
            dma((16,)),
            dma((2, 2, 8)),
            dma((2, 16)),
            dma((2, 2)),
            dma((2, 16)),
            dma((32,)),
        ],
        name="block",
        compiler_params=pltpu.CompilerParams(
            collective_id=0, has_side_effects=True, vmem_limit_bytes=58 * 1024 * 1024
        ),
    )(latents, steps, segment_ids.reshape(1, 512), mod_table, w_query, w_key, w_value)
    return out.reshape(1, 32, 4096)


def solution(mesh):
    placed = (
        P("group", "dp", None),
        P("group"),
        P(),
        P(),
        P(None, "dp"),
        P(None, "dp"),
        P(None, "dp"),
    )
    return jax.shard_map(
        per_device, mesh=mesh, in_specs=placed, out_specs=P("group", "dp", None), check_vma=False
    )
```

time: 109 us -> 93.2 us (0.86)
  the two profiles are of different devices: /device:TPU:39 before, /device:TPU:1 now
where the time goes in v2:
time: 93.2 us; the launch traced here: 93.1 us
  Pallas kernels  90.7 us (97%)
  local copies, waits for them, and re-layouts  1.67 us (2%)
    pallas_call x1, Pallas kernels, per_device(): pl.pallas_call(kernel, out_shape=jax.ShapeDtypeStruct((2, 16, 4096), BF),...  90.7 us

profile of v2, /device:TPU:1, one launch (start us, length us, event | category | flops | bytes accessed | tf_op | source)
XLA Modules:
  0.0 93.1 jit_solution(1119587019374921480)
XLA Ops:
  0.7 90.7 %block.1 = bf16[2,16,4096]{2,1,0:T(8,128)(2,1)} custom-call(bf16[1,32,6144]{2,1,0:T(8,128)(2,1)} %lat.1, s32[1]{0:T(128)S(6)} %copy.9.steps, s32[1,512]{1,0:T(1,128)} %bitcast.3, f32[16,2,6144]{2,1,0:T(2,128)} %mod.1, bf16[6144,256]{1,0:T(8,128)(2,1)} %wq.1, bf16[6144,256]{1,0:T(8,128)(2,1)} %wk.1, bf16[6144,256]{1,0:T(8,128)(2,1)} %wv.1), custom_call_target="tpu_custom_call" | custom-call | tf_op jit(solution)/shard_map/block/pallas_call | solution.py:427
  91.4 1.7 %copy.10 = bf16[1,32,4096]{2,1,0:T(8,128)(2,1)} copy(bf16[1,32,4096]{2,1,0:T(8,128)(2,1)} %bitcast.2) | data formatting | bytes 524288

commit v3 on v2

--- a/solution.py
+++ b/solution.py
@@ -19,7 +19,7 @@
 def kernel(
     lat, steps, seg, mod, wq, wk, wv, out,
     x_buf, w_buf, mod_all, mod_row, xn, own, partner, q_in, kv_in, s_buf, bias, seg_buf, o_buf, o_in,
-    xs, xr, ls, ps, pr, es, er, lx, os_, or_,
+    xs, xr, ls, ps, pr, es, er, lx, ds_, os_, or_,
 ):
     g = lax.axis_index("group")
     d = lax.axis_index("dp")
@@ -27,7 +27,11 @@
     z = d % 8
     head = g // 8
     mate = (g + 8) % 16
-    win = (g % 8 + 2 * z) % 8
+    def window_of(place):
+        core = place % 2
+        return 4 * core + (place // 2 + z + 2 * core) % 4
+
+    win = window_of(g % 8)
 
     def at_z(k):
         return {"group": g, "dp": xh * 8 + (z + k + 8) % 8}
@@ -38,11 +42,8 @@
     barrier = pltpu.get_barrier_semaphore()
     for peer in (up, down, across):
         pl.semaphore_signal(barrier, inc=1, device_id=peer, device_id_type=MESH)
-    for k in range(1, 8):
-        pl.semaphore_signal(
-            barrier, inc=1, device_id={"group": head * 8 + (g + k) % 8, "dp": d}, device_id_type=MESH
-        )
-    pl.semaphore_signal(barrier, inc=1, device_id={"group": mate, "dp": d}, device_id_type=MESH)
+    for k in range(1, 16):
+        pl.semaphore_signal(barrier, inc=1, device_id={"group": (g + k) % 16, "dp": d}, device_id_type=MESH)
 
     def block_same(k):
         return xh * 8 + (z + k + 8) % 8
@@ -67,7 +68,7 @@
     ]
     for c in loads:
         c.start()
-    pl.semaphore_wait(barrier, 11)
+    pl.semaphore_wait(barrier, 18)
 
     sends = []
 
@@ -84,9 +85,9 @@
     def relay(slot, to):
         send(x_buf.at[slot], x_buf.at[slot], to, xr.at[slot])
 
-    def relay_half(slot, part, to):
+    def relay_half(slot, part, to, second):
         cols = pl.ds(part * HALF, HALF)
-        sem = xr.at[slot] if part == 0 else xr.at[32]
+        sem = xr.at[slot] if part == 0 else xr.at[second]
         send(x_buf.at[slot, :, cols], x_buf.at[slot, :, cols], to, sem)
 
     def arrived(slot):
@@ -95,19 +96,19 @@
             device_id=up, device_id_type=MESH,
         ).wait_recv()
 
-    def arrived_half(slot, part):
+    def arrived_half(slot, part, second):
         cols = pl.ds(part * HALF, HALF)
-        sem = xr.at[slot] if part == 0 else xr.at[32]
+        sem = xr.at[slot] if part == 0 else xr.at[second]
         pltpu.make_async_remote_copy(
             src_ref=x_buf.at[slot, :, cols], dst_ref=x_buf.at[slot, :, cols], send_sem=xs.at[0], recv_sem=sem,
             device_id=up, device_id_type=MESH,
         ).wait_recv()
 
     send_own(0, across)
+    send_own(1, up)
+    send_own(1, down)
     send_own(0, up)
     send_own(0, down)
-    send_own(1, up)
-    send_own(1, down)
     send_own(1, across)
 
     loads[2].wait()
@@ -150,49 +151,81 @@
             device_id={"group": mate, "dp": d}, device_id_type=MESH,
         )
 
-    def spread(block, whose):
+    def place_of(w):
+        return 2 * ((w % 4 + 2 * (w // 4) + 8 - z) % 4) + w // 4
+
+    def reach(mid):
+        low = jnp.where(mid == 2, 0, jnp.maximum(mid - 1, 0))
+        high = jnp.where(mid == 5, 7, jnp.minimum(mid + 1, 7))
+        return low, high + 1
+
+    def rest_of(block, w):
+        return pl.ds(2 * block - 4 * (jnp.minimum(jnp.maximum(w, 1), 6) - 1), 2)
+
+    def spread(block, whose, keys=True, queries=True):
         src = own.at[head] if whose == 0 else partner
         c = g if whose == 0 else mate
         two = pl.ds(2 * block, 2)
         mid = block // 2
-
-        def to_window(i, carry):
-            w = mid + i - 2
-            cw = jnp.minimum(jnp.maximum(w, 1), 6)
-            near = jnp.logical_and(mid - cw <= 1, cw - mid <= 1)
-            use = jnp.logical_and(near, jnp.logical_and(w >= 0, w <= 7))
-            place = (w + 16 - 2 * z) % 8
+        kv_src = src.at[two, :, pl.ds(HD, 2 * HD)]
+
+        def to_window(w, carry):
+            place = place_of(w)
             here = place == g % 8
-            to = {"group": head * 8 + place, "dp": d}
-            rest = pl.ds(2 * block - 4 * (cw - 1), 2)
-            kv_src, kv_dst = src.at[two, :, pl.ds(HD, 2 * HD)], kv_in.at[c, rest]
-            q_src, q_dst = src.at[two, :, pl.ds(0, HD)], q_in.at[c, pl.ds(2 * (block % 2), 2)]
-
-            @pl.when(jnp.logical_and(use, jnp.logical_not(here)))
+            kv_dst = kv_in.at[c, rest_of(block, w)]
+
+            @pl.when(jnp.logical_not(here))
             def _():
                 pltpu.make_async_remote_copy(
                     src_ref=kv_src, dst_ref=kv_dst, send_sem=es.at[0, whose, place], recv_sem=er.at[0, c],
-                    device_id=to, device_id_type=MESH,
+                    device_id={"group": head * 8 + place, "dp": d}, device_id_type=MESH,
                 ).start()
 
-            @pl.when(jnp.logical_and(use, here))
+            @pl.when(here)
             def _():
                 pltpu.make_async_copy(kv_src, kv_dst, lx.at[0, whose]).start()
 
-            @pl.when(jnp.logical_and(i == 2, jnp.logical_not(here)))
+            return carry
+
+        if keys:
+            lax.fori_loop(*reach(mid), to_window, 0)
+        if queries:
+            place = place_of(mid)
+            here = place == g % 8
+            q_src, q_dst = src.at[two, :, pl.ds(0, HD)], q_in.at[c, pl.ds(2 * (block % 2), 2)]
+
+            @pl.when(jnp.logical_not(here))
             def _():
                 pltpu.make_async_remote_copy(
                     src_ref=q_src, dst_ref=q_dst, send_sem=es.at[1, whose, place], recv_sem=er.at[1, c],
-                    device_id=to, device_id_type=MESH,
+                    device_id={"group": head * 8 + place, "dp": d}, device_id_type=MESH,
                 ).start()
 
-            @pl.when(jnp.logical_and(i == 2, here))
+            @pl.when(here)
             def _():
                 pltpu.make_async_copy(q_src, q_dst, lx.at[1, whose]).start()
 
+    def direct_keys(block, i, w):
+        return pltpu.make_async_remote_copy(
+            src_ref=own.at[1 - head, pl.ds(2 * block, 2), :, pl.ds(HD, 2 * HD)], dst_ref=kv_in.at[g, rest_of(block, w)],
+            send_sem=ds_.at[i, w], recv_sem=er.at[0, g],
+            device_id={"group": (1 - head) * 8 + place_of(w), "dp": d}, device_id_type=MESH,
+        )
+
+    def direct_queries(block, i):
+        w = block // 2
+        return pltpu.make_async_remote_copy(
+            src_ref=own.at[1 - head, pl.ds(2 * block, 2), :, pl.ds(0, HD)],
+            dst_ref=q_in.at[g, pl.ds(2 * (block % 2), 2)], send_sem=ds_.at[i, 8], recv_sem=er.at[1, g],
+            device_id={"group": (1 - head) * 8 + place_of(w), "dp": d}, device_id_type=MESH,
+        )
+
+    def over_reach(block, call):
+        def step(w, carry):
+            call(w)
             return carry
 
-        lax.fori_loop(0, 5, to_window, 0)
+        lax.fori_loop(*reach(block // 2), step, 0)
 
     todo = []
 
@@ -210,10 +243,23 @@
                 norm(slots[i], i)
         return call
 
-    def plan(slots, blocks, before):
+    straight = [block_other(-3), block_other(3), block_same(4), block_other(4)]
+
+    def out_keys(which):
+        for i in which:
+            over_reach(straight[i], lambda w, i=i: direct_keys(straight[i], i, w).start())
+            spread(straight[i], 0, queries=False)
+
+    def out_queries(which):
+        for i in which:
+            direct_queries(straight[i], i).start()
+            spread(straight[i], 0, keys=False)
+
+    def plan(slots, blocks, before, crossed=True):
         n = len(slots)
         for at in range(0, n, 2):
-            todo.append((0.5 if at < 4 else 1.0, norms(slots, (at, at + 1), at == 6)))
+            wait = crossed and at == n - 2
+            todo.append((0.5 if at < 4 else 1.0, norms(slots, (at, at + 1), wait)))
         for which in range(3):
             todo.append((1.0, lambda which=which: project(which, slots)))
 
@@ -263,94 +309,145 @@
 
     before = blocks
     for s in range(1, 4):
-        for half in range(2):
-            a, b = same(-s, half), same(s, half)
-            arrived(a)
-            if s < 3 or half == 0:
-                relay(a, up)
-            if half == 1:
-                relay(a, across)
-            work(1.0)
-            arrived(b)
-            if s < 3 or half == 1:
-                relay(b, down)
-            if half == 1:
-                relay(b, across)
+        a, b = same(-s, 1), same(s, 1)
+        arrived(a)
+        if s < 3:
+            relay(a, up)
+        relay(a, across)
+        arrived(b)
+        if s < 3:
+            relay(b, down)
+        else:
+            relay_half(b, 0, down, 33)
+            relay_half(b, 1, down, 33)
+        relay(b, across)
+        work(2.0)
+        a, b = same(-s, 0), same(s, 0)
+        arrived(a)
+        relay(a, up)
+        arrived(b)
+        if s < 3:
+            relay(b, down)
+        if s < 3:
+            work(2.0)
+        else:
+            work(100.0)
+            chunk = [same(-s, 0), same(s, 0), same(-s, 1), same(s, 1)]
+            blocks = [block_same(-s), block_same(s)]
+            plan(chunk, blocks, before, crossed=False)
+            before = blocks
             work(1.0)
         a, b = other(-s, 0), other(s, 0)
         arrived(a)
         if s < 3:
             relay(a, up)
         else:
-            relay_half(a, 0, up)
+            relay_half(a, 0, up, 32)
+        arrived(b)
+        if s < 3:
+            relay(b, down)
+            chunk = [same(-s, 0), same(s, 0), same(-s, 1), same(s, 1), other(-s, 0), other(s, 0), other(-s, 1), other(s, 1)]
+            blocks = [block_same(-s), block_same(s), block_other(-s), block_other(s)]
+        else:
+            relay_half(b, 1, down, 32)
+            chunk = [other(-s, 0), other(s, 0), other(-s, 1), other(s, 1)]
+            blocks = [block_other(-s), block_other(s)]
+        if s < 3:
+            work(2.0)
+            plan(chunk, blocks, before)
+            before = blocks
+        else:
+            work(100.0)
+            todo.append((0.5, norms(chunk, (0, 1), False)))
+            todo.append((0.5, norms(chunk, (2, 3), True)))
+            for which in (1, 2):
+                todo.append((1.0, lambda which=which, chunk=chunk: project(which, chunk)))
+            todo.append((0.5, lambda: out_keys((0, 1))))
+            todo.append((1.0, lambda chunk=chunk: project(0, chunk)))
+            todo.append((0.5, lambda: out_queries((0, 1))))
+
+    def finish(slots, which):
+        project(1, slots)
+        project(2, slots)
+        out_keys(which)
+        project(0, slots)
+        out_queries(which)
+
+    mine, theirs = [same(4, 0), same(4, 1)], [other(4, 0), other(4, 1)]
+    work(2.0)
+    for part in range(2):
+        arrived_half(mine[1], part, 33)
+        relay_half(mine[1], part, across, 34)
         work(1.0)
-        arrived(b)
-        if s < 3:
-            relay(b, down)
-        else:
-            relay_half(b, 1, down)
-        work(1.0)
-        chunk = [same(-s, 0), same(s, 0), same(-s, 1), same(s, 1), other(-s, 0), other(s, 0), other(-s, 1), other(s, 1)]
-        blocks = [block_same(-s), block_same(s), block_other(-s), block_other(s)]
-        plan(chunk, blocks, before)
-        before = blocks
-
-    work(1.0)
-    arrived(same(4, 1))
-    relay(same(4, 1), across)
     work(100.0)
-    chunk = [same(4, 0), same(4, 1), other(4, 0), other(4, 1)]
-    blocks = [block_same(4), block_other(4)]
-    arrived(chunk[0])
-    norm(chunk[0], 0)
-    norm(chunk[1], 1)
+    arrived(mine[0])
+    norm(mine[0], 0)
+    norm(mine[1], 1)
+    finish(mine, (2,))
     out_mate(before)
-    arrived_half(chunk[2], 0)
-    arrived_half(chunk[2], 1)
-    norm(chunk[2], 2)
-    arrived(chunk[3])
-    norm(chunk[3], 3)
-    for which in range(3):
-        project(which, chunk)
-    for b in blocks:
-        swap(b).start()
-    for b in blocks:
-        spread(b, 0)
-    out_mate(blocks)
-
-    kv_whole, q_whole = own.at[0, pl.ds(0, 12), :, pl.ds(HD, 2 * HD)], own.at[0, pl.ds(0, 4), :, pl.ds(0, HD)]
-
-    def whole(i, whose, place, c):
+    arrived_half(theirs[0], 0, 32)
+    arrived_half(theirs[0], 1, 32)
+    norm(theirs[0], 0)
+    arrived_half(theirs[1], 0, 34)
+    arrived_half(theirs[1], 1, 34)
+    norm(theirs[1], 1)
+    finish(theirs, (3,))
+
+    def late(i, w):
+        n = 0
+        for b in straight:
+            low, high = reach(b // 2)
+            hit = jnp.logical_and(w >= low, w < high) if i == 0 else b // 2 == w
+            n = n + jnp.where(hit, 1, 0)
+        return n
+
+    def units(i, n, c, send_sem, recv_sem):
+        cols = pl.ds(HD, 2 * HD) if i == 0 else pl.ds(0, HD)
         return pltpu.make_async_remote_copy(
-            src_ref=(kv_whole, q_whole)[i], dst_ref=(kv_in, q_in)[i].at[c], send_sem=es.at[i, whose, place],
-            recv_sem=er.at[i, c], device_id=up, device_id_type=MESH,
+            src_ref=own.at[0, pl.ds(0, n), :, cols], dst_ref=(kv_in, q_in)[i].at[c, pl.ds(0, n)],
+            send_sem=send_sem, recv_sem=recv_sem, device_id=up, device_id_type=MESH,
         )
 
-    for whose in range(2):
-        c = (g, mate)[whose]
-        pltpu.make_async_copy(kv_whole, kv_in.at[c], lx.at[0, whose]).wait()
-        pltpu.make_async_copy(q_whole, q_in.at[c], lx.at[1, whose]).wait()
+    def local_units(i, n, c, sem):
+        cols = pl.ds(HD, 2 * HD) if i == 0 else pl.ds(0, HD)
+        return pltpu.make_async_copy(own.at[0, pl.ds(0, n), :, cols], (kv_in, q_in)[i].at[c, pl.ds(0, n)], sem)
+
+    WHOLE = (12, 4)
+
+    for i in range(2):
+        local_units(i, WHOLE[i], g, lx.at[i, 0]).wait()
+        n = late(i, win)
+        for j in range(5):
+            @pl.when(n == j)
+            def _(i=i, j=j):
+                if WHOLE[i] > 2 * j:
+                    local_units(i, WHOLE[i] - 2 * j, mate, lx.at[i, 1]).wait()
+                if 0 < 2 * j <= WHOLE[i]:
+                    units(i, 2 * j, mate, es.at[i, 0, 0], er.at[i, mate]).wait_recv()
     for k in range(1, 8):
         c = (g + k) % 8
         for side in range(2):
             for i in range(2):
-                whole(i, 0, 0, c + 8 * side).wait_recv()
-
-    scale = 1.0 / math.sqrt(HD)
-
-    def attend(b):
+                units(i, WHOLE[i], c + 8 * side, es.at[i, 0, 0], er.at[i, c + 8 * side]).wait_recv()
+
+    scale = math.log2(math.e) / math.sqrt(HD)
+
+    def score(b):
         q = q_in[4 * b : 4 * b + 4].reshape(256, HD)
         best = jnp.full((256, 1), NEG, F32)
         for kb in range(b + 1):
             keys = kv_in[4 * kb : 4 * kb + 4, :, :, 0:HD].reshape(768, HD)
             sc = lax.dot_general(q, keys, (((1,), (1,)), ((), ())), preferred_element_type=F32)
             sc = sc * scale + bias[1 if kb == b else 0]
-            s_buf[:, 768 * kb : 768 * kb + 768] = sc
+            s_buf[b % 2, :, 768 * kb : 768 * kb + 768] = sc
             best = jnp.maximum(best, jnp.max(sc, axis=-1, keepdims=True))
+        return best
+
+    def attend(b, best):
         total = jnp.zeros((256, 1), F32)
         acc = jnp.zeros((256, HD), F32)
         for kb in range(b + 1):
-            p = jnp.exp(s_buf[:, 768 * kb : 768 * kb + 768] - best)
+            p = jnp.exp2(s_buf[b % 2, :, 768 * kb : 768 * kb + 768] - best)
             total = total + jnp.sum(p, axis=-1, keepdims=True)
             vals = kv_in[4 * kb : 4 * kb + 4, :, :, HD : 2 * HD].reshape(768, HD)
             acc = acc + jnp.dot(p.astype(BF), vals, preferred_element_type=F32)
@@ -382,15 +479,17 @@
                     lc.start()
                     lc.wait()
 
-    attend(3)
-    for b in (2, 1, 0):
-        attend(b)
-        send_home(b + 1)
-    send_home(0)
+    best = score(3)
+    for b in (3, 2, 1, 0):
+        attend(b, best)
+        if b > 0:
+            best = score(b - 1)
+        send_home(b)
 
     for hd in range(32):
         src_d = hd // 2
-        src_g = (hd % 2) * 8 + (d // 2 + 16 - 2 * (src_d % 8)) % 8
+        src_w = d // 2
+        src_g = (hd % 2) * 8 + 2 * ((src_w % 4 + 2 * (src_w // 4) + 8 - src_d % 8) % 4) + src_w // 4
         remote = jnp.logical_or(src_g != g, src_d != d)
 
         @pl.when(remote)
@@ -405,13 +504,23 @@
 
     for c in sends:
         c.wait_send()
-    for b in range(16):
-        swap(b).wait_send()
+    for k in range(-3, 4):
+        swap(block_same(k)).wait_send()
+    for k in range(-2, 3):
+        swap(block_other(k)).wait_send()
+    for i, b in enumerate(straight):
+        over_reach(b, lambda w, b=b, i=i: direct_keys(b, i, w).wait_send())
+        direct_queries(b, i).wait_send()
     for k in range(1, 8):
-        w = (g + k) % 8
-        for whose in range(2):
-            for i in range(2):
-                whole(i, whose, w, 0).wait_send()
+        place = (g + k) % 8
+        for i in range(2):
+            units(i, WHOLE[i], 0, es.at[i, 0, place], er.at[i, 0]).wait_send()
+            n = late(i, window_of(place))
+            for j in range(5):
+                if WHOLE[i] > 2 * j:
+                    @pl.when(n == j)
+                    def _(i=i, j=j, place=place):
+                        units(i, WHOLE[i] - 2 * j, 0, es.at[i, 1, place], er.at[i, 0]).wait_send()
     for half in range(2):
         for c in range(16):
             @pl.when(away(c, half))
@@ -439,19 +548,20 @@
             vmem((32, 16, 3 * HD), BF),
             vmem((16, 4, 16, HD), BF),
             vmem((16, 12, 16, 2 * HD), BF),
-            vmem((256, 3072), F32),
+            vmem((2, 256, 3072), F32),
             vmem((2, 256, 768), F32),
             vmem((1, 512), jnp.int32),
             vmem((16, 4, 16, HD), BF),
             vmem((2, 16, 4096), BF),
             dma((48,)),
-            dma((33,)),
+            dma((35,)),
             dma((9,)),
             dma((16,)),
             dma((16,)),
             dma((2, 2, 8)),
             dma((2, 16)),
             dma((2, 2)),
+            dma((4, 9)),
             dma((2, 16)),
             dma((32,)),
         ],

time: 93.2 us -> 90.4 us (0.970)
  Pallas kernels: 90.7 us -> 87.9 us
    pallas_call x1, Pallas kernels: 90.7 us -> 87.9 us  [per_device(): pl.pallas_call(kernel, out_shape=jax.ShapeDtypeStruct((2, 16, 4096), BF),...]
where the time goes in v3:
time: 90.4 us; the launch traced here: 90.3 us
  Pallas kernels  87.9 us (97%)
  local copies, waits for them, and re-layouts  1.67 us (2%)
    pallas_call x1, Pallas kernels, per_device(): pl.pallas_call(kernel, out_shape=jax.ShapeDtypeStruct((2, 16, 4096), BF),...  87.9 us

profile of v3, /device:TPU:1, one launch (start us, length us, event | category | flops | bytes accessed | tf_op | source)
XLA Modules:
  0.0 90.3 jit_solution(15249654966464457386)
XLA Ops:
  0.7 87.9 %block.1 = bf16[2,16,4096]{2,1,0:T(8,128)(2,1)} custom-call(bf16[1,32,6144]{2,1,0:T(8,128)(2,1)} %lat.1, s32[1]{0:T(128)S(6)} %copy.9.steps, s32[1,512]{1,0:T(1,128)} %bitcast.3, f32[16,2,6144]{2,1,0:T(2,128)} %mod.1, bf16[6144,256]{1,0:T(8,128)(2,1)} %wq.1, bf16[6144,256]{1,0:T(8,128)(2,1)} %wk.1, bf16[6144,256]{1,0:T(8,128)(2,1)} %wv.1), custom_call_target="tpu_custom_call" | custom-call | tf_op jit(solution)/shard_map/block/pallas_call | solution.py:536
  88.6 1.7 %copy.10 = bf16[1,32,4096]{2,1,0:T(8,128)(2,1)} copy(bf16[1,32,4096]{2,1,0:T(8,128)(2,1)} %bitcast.2) | data formatting | bytes 524288

commit v4 on v3

--- a/solution.py
+++ b/solution.py
@@ -318,8 +318,7 @@
         if s < 3:
             relay(b, down)
         else:
-            relay_half(b, 0, down, 33)
-            relay_half(b, 1, down, 33)
+            relay(b, down)
         relay(b, across)
         work(2.0)
         a, b = same(-s, 0), same(s, 0)
@@ -359,7 +358,7 @@
         else:
             work(100.0)
             todo.append((0.5, norms(chunk, (0, 1), False)))
-            todo.append((0.5, norms(chunk, (2, 3), True)))
+            todo.append((0.5, norms(chunk, (2, 3), False)))
             for which in (1, 2):
                 todo.append((1.0, lambda which=which, chunk=chunk: project(which, chunk)))
             todo.append((0.5, lambda: out_keys((0, 1))))
@@ -374,12 +373,12 @@
         out_queries(which)
 
     mine, theirs = [same(4, 0), same(4, 1)], [other(4, 0), other(4, 1)]
-    work(2.0)
-    for part in range(2):
-        arrived_half(mine[1], part, 33)
-        relay_half(mine[1], part, across, 34)
-        work(1.0)
+    arrived(other(-3, 1))
+    relay_half(other(-3, 1), 0, up, 34)
+    arrived(other(3, 1))
+    relay_half(other(3, 1), 1, down, 34)
     work(100.0)
+    arrived(mine[1])
     arrived(mine[0])
     norm(mine[0], 0)
     norm(mine[1], 1)

time: 90.4 us -> 88.8 us (0.982)
  Pallas kernels: 87.9 us -> 86.3 us
    pallas_call x1, Pallas kernels: 87.9 us -> 86.3 us  [per_device(): pl.pallas_call(kernel, out_shape=jax.ShapeDtypeStruct((2, 16, 4096), BF),...]
where the time goes in v4:
time: 88.8 us; the launch traced here: 88.7 us
  Pallas kernels  86.3 us (97%)
  local copies, waits for them, and re-layouts  1.67 us (2%)
    pallas_call x1, Pallas kernels, per_device(): pl.pallas_call(kernel, out_shape=jax.ShapeDtypeStruct((2, 16, 4096), BF),...  86.3 us

profile of v4, /device:TPU:1, one launch (start us, length us, event | category | flops | bytes accessed | tf_op | source)
XLA Modules:
  0.0 88.7 jit_solution(11257032469158646801)
XLA Ops:
  0.7 86.3 %block.1 = bf16[2,16,4096]{2,1,0:T(8,128)(2,1)} custom-call(bf16[1,32,6144]{2,1,0:T(8,128)(2,1)} %lat.1, s32[1]{0:T(128)S(6)} %copy.9.steps, s32[1,512]{1,0:T(1,128)} %bitcast.3, f32[16,2,6144]{2,1,0:T(2,128)} %mod.1, bf16[6144,256]{1,0:T(8,128)(2,1)} %wq.1, bf16[6144,256]{1,0:T(8,128)(2,1)} %wk.1, bf16[6144,256]{1,0:T(8,128)(2,1)} %wv.1), custom_call_target="tpu_custom_call" | custom-call | tf_op jit(solution)/shard_map/block/pallas_call | solution.py:535
  87.0 1.7 %copy.10 = bf16[1,32,4096]{2,1,0:T(8,128)(2,1)} copy(bf16[1,32,4096]{2,1,0:T(8,128)(2,1)} %bitcast.2) | data formatting | bytes 524288

commit v5 on v4

--- a/solution.py
+++ b/solution.py
@@ -243,7 +243,7 @@
                 norm(slots[i], i)
         return call
 
-    straight = [block_other(-3), block_other(3), block_same(4), block_other(4)]
+    straight = [block_other(-3), block_other(3), block_same(4), block_other(4), block_same(-3), block_same(3)]
 
     def out_keys(which):
         for i in which:
@@ -255,10 +255,10 @@
             direct_queries(straight[i], i).start()
             spread(straight[i], 0, keys=False)
 
-    def plan(slots, blocks, before, crossed=True):
+    def plan(slots, blocks, before):
         n = len(slots)
         for at in range(0, n, 2):
-            wait = crossed and at == n - 2
+            wait = at == n - 2
             todo.append((0.5 if at < 4 else 1.0, norms(slots, (at, at + 1), wait)))
         for which in range(3):
             todo.append((1.0, lambda which=which: project(which, slots)))
@@ -332,9 +332,14 @@
         else:
             work(100.0)
             chunk = [same(-s, 0), same(s, 0), same(-s, 1), same(s, 1)]
-            blocks = [block_same(-s), block_same(s)]
-            plan(chunk, blocks, before, crossed=False)
-            before = blocks
+            todo.append((0.5, norms(chunk, (0, 1), False)))
+            todo.append((0.5, norms(chunk, (2, 3), False)))
+            for which in (1, 2):
+                todo.append((1.0, lambda which=which, chunk=chunk: project(which, chunk)))
+            todo.append((0.5, lambda: out_keys((4, 5))))
+            todo.append((1.0, lambda chunk=chunk: project(0, chunk)))
+            todo.append((0.5, lambda: out_queries((4, 5))))
+            todo.append((0.5, lambda before=before: out_mate(before)))
             work(1.0)
         a, b = other(-s, 0), other(s, 0)
         arrived(a)
@@ -383,7 +388,6 @@
     norm(mine[0], 0)
     norm(mine[1], 1)
     finish(mine, (2,))
-    out_mate(before)
     arrived_half(theirs[0], 0, 32)
     arrived_half(theirs[0], 1, 32)
     norm(theirs[0], 0)
@@ -416,7 +420,7 @@
     for i in range(2):
         local_units(i, WHOLE[i], g, lx.at[i, 0]).wait()
         n = late(i, win)
-        for j in range(5):
+        for j in range(7):
             @pl.when(n == j)
             def _(i=i, j=j):
                 if WHOLE[i] > 2 * j:
@@ -503,9 +507,8 @@
 
     for c in sends:
         c.wait_send()
-    for k in range(-3, 4):
+    for k in range(-2, 3):
         swap(block_same(k)).wait_send()
-    for k in range(-2, 3):
         swap(block_other(k)).wait_send()
     for i, b in enumerate(straight):
         over_reach(b, lambda w, b=b, i=i: direct_keys(b, i, w).wait_send())
@@ -515,7 +518,7 @@
         for i in range(2):
             units(i, WHOLE[i], 0, es.at[i, 0, place], er.at[i, 0]).wait_send()
             n = late(i, window_of(place))
-            for j in range(5):
+            for j in range(7):
                 if WHOLE[i] > 2 * j:
                     @pl.when(n == j)
                     def _(i=i, j=j, place=place):
@@ -560,7 +563,7 @@
             dma((2, 2, 8)),
             dma((2, 16)),
             dma((2, 2)),
-            dma((4, 9)),
+            dma((6, 9)),
             dma((2, 16)),
             dma((32,)),
         ],

time: 88.8 us -> 88.7 us (level)
  no operation moved by 1% of the time
where the time goes in v5:
time: 88.7 us; the launch traced here: 88.6 us
  Pallas kernels  86.3 us (97%)
  local copies, waits for them, and re-layouts  1.67 us (2%)
    pallas_call x1, Pallas kernels, per_device(): pl.pallas_call(kernel, out_shape=jax.ShapeDtypeStruct((2, 16, 4096), BF),...  86.3 us

profile of v5, /device:TPU:1, one launch (start us, length us, event | category | flops | bytes accessed | tf_op | source)
XLA Modules:
  0.0 88.6 jit_solution(9038005152486111678)
XLA Ops:
  0.7 86.3 %block.1 = bf16[2,16,4096]{2,1,0:T(8,128)(2,1)} custom-call(bf16[1,32,6144]{2,1,0:T(8,128)(2,1)} %lat.1, s32[1]{0:T(128)S(6)} %copy.9.steps, s32[1,512]{1,0:T(1,128)} %bitcast.3, f32[16,2,6144]{2,1,0:T(2,128)} %mod.1, bf16[6144,256]{1,0:T(8,128)(2,1)} %wq.1, bf16[6144,256]{1,0:T(8,128)(2,1)} %wk.1, bf16[6144,256]{1,0:T(8,128)(2,1)} %wv.1), custom_call_target="tpu_custom_call" | custom-call | tf_op jit(solution)/shard_map/block/pallas_call | solution.py:538
  87.0 1.7 %copy.10 = bf16[1,32,4096]{2,1,0:T(8,128)(2,1)} copy(bf16[1,32,4096]{2,1,0:T(8,128)(2,1)} %bitcast.2) | data formatting | bytes 524288
